TPU v7x, 32 devices: a whole 2x2x4 slice. The times are simulated.
32 devices in a mesh: groups: 2 (over y), tm: 4 (over z), dp: 2 (over x), width: 2 (over core).
Axes of the slice: x: 2, y: 2, z: 4, core: 2. Of those that a mesh axis runs over, the one named last changes fastest.
Arguments:
- clips: bfloat16 [4, 16, 8, 64, 128], P(('groups', 'dp'), 'tm', 'width'), parts along dimension 0, may hold values from -16.5 to 16.5
- gain: float32 [128], replicated, may hold values from 0.5 to 1.5
- bias: float32 [128], replicated, may hold values from -3 to 3
- weight: bfloat16 [3456, 256], replicated, may hold values from -0.109375 to 0.109375
- cotangent: bfloat16 [4, 16, 8, 64, 256], P(('groups', 'dp'), 'tm', 'width'), parts along dimension 0, may hold values from -6 to 6
Outputs:
- output: bfloat16 [4, 16, 8, 64, 256], P(('groups', 'dp'), 'tm', 'width'), parts along dimension 0
- grad_weight: float32 [6912, 256], P(('groups', 'tm', 'dp'), 'width'), parts along dimension 0
- grad_gain: float32 [256], P('groups'), parts along dimension 0
- grad_bias: float32 [256], P('groups'), parts along dimension 0
There are 2 independent parts, one for each index of `groups`. A program takes and returns all parts, laid end to end along the dimension named above; an argument that names none is the same for every part. Nothing has to cross between parts.
All inputs are finite; a program needn't handle non-finite values.
Results may differ from a plain program's by a relative error of at most 0.0049.
Values may be sent and summed in bfloat16 or wider, within the bound.
No kernel may reach another device: no remote copies, remote signals or barrier semaphores. Data moves between devices by JAX's collectives and lax.ppermute only.
A program may use at most 64 MiB of HBM per device.

v0:
```python
import jax
import jax.numpy as jnp
from jax import lax
from jax.sharding import PartitionSpec as P

GROUPS = 32


def prefix(value, axis, join, neutral):
    count, mine = (lax.axis_size(axis), lax.axis_index(axis))
    pieces = jax.tree.map(lambda part: lax.all_gather(part, axis), value)
    total = jax.tree.map(
        lambda part, zero: jnp.full_like(part, 0) + jnp.asarray(zero, part.dtype), value, neutral
    )

    def lap(position, total):
        longer = join(total, jax.tree.map(lambda part: part[position], pieces))
        return jax.tree.map(lambda new, old: jnp.where(position < mine, new, old), longer, total)

    return lax.fori_loop(0, count - 1, lap, total)


def with_halo(value, sides, width):
    for axis, dim in sides:
        devices, length = (lax.axis_size(axis), value.shape[dim])
        up = [(i, (i + 1) % devices) for i in range(devices - 1)]
        down = [(j, i) for i, j in up]
        last = lax.slice_in_dim(value, length - width, length, axis=dim)
        first = lax.slice_in_dim(value, 0, width, axis=dim)
        before = lax.ppermute(last, axis, up)
        after = lax.ppermute(first, axis, down)
        value = jnp.concatenate([before, value, after], axis=dim)
    return value


def from_behind(value, axis, steps):
    count = lax.axis_size(axis)
    first, last = (max(0, -steps), min(count, count - steps))
    return lax.ppermute(value, axis, [(source, source + steps) for source in range(first, last)])


def add_pair(earlier, later):
    return (earlier[0] + later[0], earlier[1] + later[1])


def body(clips, gain, bias, weight, cotangent):
    frames_in = clips[0]
    frame_count, row_count, col_count, chan_in = frames_in.shape
    chan_out = weight.shape[1]
    per_group = chan_in // GROUPS
    values = frames_in.astype(jnp.float32)
    grouped = values.reshape(frame_count, row_count, col_count, GROUPS, per_group)
    local_first = jnp.sum(grouped, axis=(1, 2, 4))
    local_square = jnp.sum(grouped * grouped, axis=(1, 2, 4))
    total_first, total_square = lax.psum((local_first, local_square), "width")
    zero_row = jnp.zeros((GROUPS,), jnp.float32)
    before_first, before_square = prefix(
        (jnp.sum(total_first, axis=0), jnp.sum(total_square, axis=0)),
        "tm",
        add_pair,
        (zero_row, zero_row),
    )
    first_sum = before_first + jnp.cumsum(total_first, axis=0)
    square_sum = before_square + jnp.cumsum(total_square, axis=0)
    frame_start = (lax.axis_index("tm") * frame_count).astype(jnp.float32)
    count = (frame_start + jnp.arange(frame_count, dtype=jnp.float32) + 1.0) * float(
        row_count * lax.axis_size("width") * col_count * per_group
    )
    mean = first_sum / count[:, None]
    variance = square_sum / count[:, None] - mean * mean
    inverse = lax.rsqrt(variance + 1e-05)
    normed = ((grouped - mean[:, None, None, :, None]) * inverse[:, None, None, :, None]).reshape(
        frame_count, row_count, col_count, chan_in
    )
    act = normed * gain + bias
    sigma = jax.nn.sigmoid(act)
    hidden = (act * sigma).astype(jnp.bfloat16)
    hidden_rows = with_halo(hidden, (("width", 1),), 1)
    earlier = from_behind(hidden_rows[frame_count - 2 :], "tm", 1)
    padded = jnp.pad(
        jnp.concatenate([earlier, hidden_rows], axis=0), ((0, 0), (0, 0), (1, 1), (0, 0))
    )
    pieces = []
    for lag_t in range(3):
        for row_off in range(3):
            for col_off in range(3):
                pieces.append(
                    padded[
                        lag_t : lag_t + frame_count,
                        row_off : row_off + row_count,
                        col_off : col_off + col_count,
                    ].reshape(-1, chan_in)
                )
    patches = jnp.concatenate(pieces, axis=1)
    output = jnp.dot(patches, weight, preferred_element_type=jnp.float32).astype(jnp.bfloat16)
    output = output.reshape(1, frame_count, row_count, col_count, chan_out)
    cot_local = cotangent[0]
    cot_rows = with_halo(cot_local, (("width", 1),), 1)
    later = from_behind(cot_rows[:2], "tm", -1)
    cot_padded = jnp.pad(
        jnp.concatenate([cot_rows, later], axis=0), ((0, 0), (0, 0), (1, 1), (0, 0))
    )
    kernel_taps = weight.reshape(27, chan_in, chan_out)
    grad_hidden = jnp.zeros((frame_count * row_count * col_count, chan_in), jnp.float32)
    for lag_t in range(3):
        for row_off in range(3):
            for col_off in range(3):
                tap_index = (lag_t * 3 + row_off) * 3 + col_off
                window = cot_padded[
                    2 - lag_t : 2 - lag_t + frame_count,
                    2 - row_off : 2 - row_off + row_count,
                    2 - col_off : 2 - col_off + col_count,
                ].reshape(-1, chan_out)
                grad_hidden = grad_hidden + lax.dot_general(
                    window,
                    kernel_taps[tap_index],
                    (((1,), (1,)), ((), ())),
                    preferred_element_type=jnp.float32,
                )
    grad_hidden = grad_hidden.reshape(frame_count, row_count, col_count, chan_in)
    grad_act = grad_hidden * sigma * (1.0 + act * (1.0 - sigma))
    grad_gain, grad_bias = lax.psum(
        (jnp.sum(grad_act * normed, axis=(0, 1, 2)), jnp.sum(grad_act, axis=(0, 1, 2))),
        ("tm", "dp", "width"),
    )
    cot_flat = cot_local.reshape(-1, chan_out)
    partial_rows = lax.psum_scatter(
        lax.dot_general(
            patches, cot_flat, (((0,), (0,)), ((), ())), preferred_element_type=jnp.float32
        ),
        ("tm", "dp"),
        scatter_dimension=0,
        tiled=True,
    )
    grad_weight = lax.psum_scatter(partial_rows, "width", scatter_dimension=1, tiled=True)
    return (output, grad_weight, grad_gain, grad_bias)


def solution(mesh):
    return jax.shard_map(
        body,
        mesh=mesh,
        in_specs=(
            P(("groups", "dp"), "tm", "width", None, None),
            P(),
            P(),
            P(),
            P(("groups", "dp"), "tm", "width", None, None),
        ),
        out_specs=(
            P(("groups", "dp"), "tm", "width", None, None),
            P(("groups", "tm", "dp"), "width"),
            P("groups"),
            P("groups"),
        ),
        check_vma=False,
    )
```

profile of v0, /device:TPU:0, one launch (start us, length us, event | category | flops | bytes accessed | tf_op | source)
XLA Modules:
  0.0 179.6 jit_solution(5625925412675377033)
XLA Ops:
  7.2 1.1 multiply_reduce_fusion.1
  8.8 2.6 %all-reduce.6 = (f32[4,32]{1,0:T(4,128)S(1)}, f32[4,32]{1,0:T(4,128)S(1)}) all-reduce(f32[4,32]{1,0:T(4,128)S(1)} %reduce_sum.70, f32[4,32]{1,0:T(4,128)S(1)} %reduce_sum.74), channel_id=1, replica_groups=mesh['groups'=2,'tm'=4,'dp'=2,'width'=2] {'width'}, use_global_device_ids=true, to_apply=%region_2.0 | all-reduce | flops 256 | bytes 2048 | tf_op jit(solution)/shard_map/psum | solution.py:55
  11.4 1.2 dynamic-slice
  13.8 13.3 %all-reduce.5 = (f32[128]{0:T(128)S(1)}, f32[128]{0:T(128)S(1)}) all-reduce(f32[128]{0:T(128)S(1)} %dynamic-update-slice, f32[128]{0:T(128)S(1)} %dynamic-update-slice.1), channel_id=2, replica_groups=mesh['groups'=2,'tm'=4,'dp'=2,'width'=2] {'tm'}, use_global_device_ids=true, to_apply=%add.2 | all-reduce | flops 256 | bytes 2048
  27.8 1.2 multiply_convert_fusion.1
  29.0 1.3 collective-permute-start.1
  30.3 3.0 %collective-permute-start = (bf16[4,1,64,128]{3,2,1,0:T(8,128)(2,1)S(1)}, bf16[4,1,64,128]{3,2,1,0:T(8,128)(2,1)S(1)}, u32[]{:S(2)}, u32[]{:S(2)}) collective-permute-start(bf16[4,1,64,128]{3,2,1,0:T(8,128)(2,1)S(1)} %get-tuple-element.217), channel_id=1, source_target_pairs={{0,1},{2,3},{4,5},{6,7},{8,9},{10,11},{12,13},{14,15},{16,17},{18,... | collective-permute-start | bytes 196616 | tf_op jit(solution)/shard_map/ppermute | solution.py:30
  34.4 1.3 collective-permute-start.4
  35.7 3.0 %collective-permute-start.3 = (bf16[4,1,64,256]{3,2,1,0:T(8,128)(2,1)S(1)}, bf16[4,1,64,256]{3,2,1,0:T(8,128)(2,1)S(1)}, u32[]{:S(2)}, u32[]{:S(2)}) collective-permute-start(bf16[4,1,64,256]{3,2,1,0:T(8,128)(2,1)S(1)} %get-tuple-element.213), channel_id=1, source_target_pairs={{0,1},{2,3},{4,5},{6,7},{8,9},{10,11},{12,13},{14,15},{16,17},{18,... | collective-permute-start | bytes 393224 | tf_op jit(solution)/shard_map/ppermute | solution.py:30
  38.8 1.3 collective-permute-start.2
  40.2 1.3 collective-permute-start.5
  41.6 2.4 %collective-permute-done.2 = bf16[2,6,64,128]{3,2,1,0:T(8,128)(2,1)S(1)} collective-permute-done((bf16[2,6,64,128]{3,2,1,0:T(8,128)(2,1)S(1)}, bf16[2,6,64,128]{3,2,1,0:T(8,128)(2,1)S(1)}, u32[]{:S(2)}, u32[]{:S(2)}) %collective-permute-start.2) | collective-permute-done | bytes 196640 | tf_op jit(solution)/shard_map/ppermute | solution.py:39
  48.7 2.9 %copy-done.5 = bf16[1024,3456]{1,0:T(8,128)(2,1)} copy-done((bf16[1024,3456]{1,0:T(8,128)(2,1)}, bf16[1024,3456]{1,0:T(8,128)(2,1)S(1)}, u32[]{:S(2)}) %copy-start.5) | copy-done | bytes 7077912
  51.6 3.9 %fusion.43 = f32[3456,256]{1,0:T(8,128)} fusion(bf16[1024,3456]{1,0:T(8,128)(2,1)S(1)} %constant_dynamic-update-slice_fusion, bf16[1024,256]{1,0:T(8,128)(2,1)S(1)} %bitcast.120), kind=kOutput, calls=%fused_computation.158 | convolution fusion | flops 1811939328 | bytes 11141120 | tf_op jit(solution)/shard_map/dot_general | solution.py:128
  55.8 6.3 %convolution_convert_fusion = bf16[1024,256]{1,0:T(8,128)(2,1)} fusion(bf16[1024,3456]{1,0:T(8,128)(2,1)} %copy-done.5, bf16[3456,256]{1,0:T(8,128)(2,1)} %param.10), kind=kOutput, calls=%fused_computation.4 | convolution fusion | flops 1812201472 | bytes 9371648 | tf_op jit(solution)/shard_map/dot_general | solution.py:95
  62.3 2.6 %pad_slice_fusion.20 = (bf16[4,4,64,256]{3,2,1,0:T(8,128)(2,1)S(1)}, bf16[4,4,64,256]{3,2,1,0:T(8,128)(2,1)S(1)}, bf16[4,4,64,256]{3,2,1,0:T(8,128)(2,1)S(1)}, b...) fusion(bf16[6,6,64,256]{3,2,1,0:T(8,128)(2,1)S(1)} %pad_maximum, ...), kind=kLoop, calls=%fused_computation.137 | loop fusion | bytes 8519680 | tf_op jit(solution)/shard_map/slice | solution.py:109
  66.1 2.1 %pad_slice_fusion.19 = (bf16[4,4,64,256]{3,2,1,0:T(8,128)(2,1)}, bf16[4,4,64,256]{3,2,1,0:T(8,128)(2,1)S(1)}, bf16[4,4,64,256]{3,2,1,0:T(8,128)(2,1)S(1)}, bf16[...) fusion(bf16[6,6,64,256]{3,2,1,0:T(8,128)(2,1)S(1)} %pad_maximum, ...), kind=kLoop, calls=%fused_computation.136 | loop fusion | bytes 6946816 | tf_op jit(solution)/shard_map/slice | solution.py:109
  74.0 60.9 %reduce-scatter.3.cloned.1.call-done = f32[432,256]{1,0:T(8,128)} async-done(((f32[3456,256]{1,0:T(8,128)}), f32[432,256]{1,0:T(8,128)}) %reduce-scatter.3.cloned.1.call-update) | async-done | bytes 442384 | tf_op jit(solution)/shard_map/reduce_scatter | solution.py:127
  134.9 1.2 fusion.8
  136.1 1.1 convolution_add_fusion.3
  137.2 1.1 convolution_add_fusion.2
  138.4 1.1 convolution_add_fusion.1
  139.5 1.3 fusion.38
  140.8 31.9 %all-reduce.4 = (f32[128]{0:T(128)}, f32[128]{0:T(128)}) all-reduce(f32[128]{0:T(128)S(1)} %get-tuple-element.138, f32[128]{0:T(128)S(1)} %get-tuple-element.137), channel_id=1, replica_groups=mesh['groups'=2,'tm'=4,'dp'=2,'width'=2] {'tm','dp','width'}, use_global_device_ids=true, to_apply=%region_15.16 | all-reduce | flops 256 | bytes 2048 | tf_op jit(solution)/shard_map/psum | solution.py:122
  (112 shorter events, 14.7 us)
Async XLA Ops:
  7.2 33.0 %copy-start = (bf16[1,4,4,64,256]{4,3,2,1,0:T(8,128)(2,1)S(1)}, bf16[1,4,4,64,256]{4,3,2,1,0:T(8,128)(2,1)}, u32[]{:S(2)}) copy-start(bf16[1,4,4,64,256]{4,3,2,1,0:T(8,128)(2,1)} %param.11) | copy-start | bytes 1572868
  7.2 127.7 %reduce-scatter.3.cloned.1.call-start = ((), (), s32[]{:S(2)}) async-start(), calls=%async_computation.2 | async-start | bytes 3981312 | tf_op jit(solution)/shard_map/reduce_scatter | solution.py:127
  29.0 9.7 %collective-permute-start.1 = (bf16[4,1,64,128]{3,2,1,0:T(8,128)(2,1)S(1)}, bf16[4,1,64,128]{3,2,1,0:T(8,128)(2,1)S(1)}, u32[]{:S(2)}, u32[]{:S(2)}) collective-permute-start(bf16[4,1,64,128]{3,2,1,0:T(8,128)(2,1)S(1)} %get-tuple-element.218), channel_id=1, source_target_pairs={{1,0},{3,2},{5,4},{7,6},{9,8},{11,10},{13,12},{15,14},{17,16},{19,... | collective-permute-start | bytes 196616 | tf_op jit(solution)/shard_map/ppermute | solution.py:31
  30.3 8.4 %collective-permute-start = (bf16[4,1,64,128]{3,2,1,0:T(8,128)(2,1)S(1)}, bf16[4,1,64,128]{3,2,1,0:T(8,128)(2,1)S(1)}, u32[]{:S(2)}, u32[]{:S(2)}) collective-permute-start(bf16[4,1,64,128]{3,2,1,0:T(8,128)(2,1)S(1)} %get-tuple-element.217), channel_id=1, source_target_pairs={{0,1},{2,3},{4,5},{6,7},{8,9},{10,11},{12,13},{14,15},{16,17},{18,... | collective-permute-start | bytes 196616 | tf_op jit(solution)/shard_map/ppermute | solution.py:30
  34.4 5.8 %collective-permute-start.4 = (bf16[4,1,64,256]{3,2,1,0:T(8,128)(2,1)S(1)}, bf16[4,1,64,256]{3,2,1,0:T(8,128)(2,1)S(1)}, u32[]{:S(2)}, u32[]{:S(2)}) collective-permute-start(bf16[4,1,64,256]{3,2,1,0:T(8,128)(2,1)S(1)} %get-tuple-element.214), channel_id=1, source_target_pairs={{1,0},{3,2},{5,4},{7,6},{9,8},{11,10},{13,12},{15,14},{17,16},{19,... | collective-permute-start | bytes 393224 | tf_op jit(solution)/shard_map/ppermute | solution.py:31
  35.7 4.5 %collective-permute-start.3 = (bf16[4,1,64,256]{3,2,1,0:T(8,128)(2,1)S(1)}, bf16[4,1,64,256]{3,2,1,0:T(8,128)(2,1)S(1)}, u32[]{:S(2)}, u32[]{:S(2)}) collective-permute-start(bf16[4,1,64,256]{3,2,1,0:T(8,128)(2,1)S(1)} %get-tuple-element.213), channel_id=1, source_target_pairs={{0,1},{2,3},{4,5},{6,7},{8,9},{10,11},{12,13},{14,15},{16,17},{18,... | collective-permute-start | bytes 393224 | tf_op jit(solution)/shard_map/ppermute | solution.py:30
  38.8 5.3 %collective-permute-start.2 = (bf16[2,6,64,128]{3,2,1,0:T(8,128)(2,1)S(1)}, bf16[2,6,64,128]{3,2,1,0:T(8,128)(2,1)S(1)}, u32[]{:S(2)}, u32[]{:S(2)}) collective-permute-start(bf16[2,6,64,128]{3,2,1,0:T(8,128)(2,1)S(1)} %pad_maximum_fusion.7), channel_id=1, source_target_pairs={{0,4},{4,8},{8,12},{1,5},{5,9},{9,13},{2,6},{6,10},{10,14},{3,7},{... | collective-permute-start | bytes 589832 | tf_op jit(solution)/shard_map/ppermute | solution.py:39
  40.2 21.9 %collective-permute-start.5 = (bf16[2,6,64,256]{3,2,1,0:T(8,128)(2,1)S(1)}, bf16[2,6,64,256]{3,2,1,0:T(8,128)(2,1)S(1)}, u32[]{:S(2)}, u32[]{:S(2)}) collective-permute-start(bf16[2,6,64,256]{3,2,1,0:T(8,128)(2,1)S(1)} %pad_maximum_fusion.3), channel_id=1, source_target_pairs={{4,0},{8,4},{12,8},{5,1},{9,5},{13,9},{6,2},{10,6},{14,10},{7,3},{... | collective-permute-start | bytes 1179656 | tf_op jit(solution)/shard_map/ppermute | solution.py:39
  46.4 1.0 copy-start.1
  46.4 1.0 copy-start.6
  46.4 1.0 copy-start.7
  48.7 2.9 %copy-start.5 = (bf16[1024,3456]{1,0:T(8,128)(2,1)}, bf16[1024,3456]{1,0:T(8,128)(2,1)S(1)}, u32[]{:S(2)}) copy-start(bf16[1024,3456]{1,0:T(8,128)(2,1)S(1)} %constant_dynamic-update-slice_fusion) | copy-start | bytes 21233668
  55.6 117.2 %reduce-scatter.5.cloned.1.call-start = ((), (), s32[]{:S(2)}) async-start(), calls=%async_computation.3 | async-start | bytes 663552 | tf_op jit(solution)/shard_map/reduce_scatter | solution.py:135
  62.3 2.7 %copy-start.4 = (bf16[3456,256]{1,0:T(8,128)(2,1)S(1)}, bf16[3456,256]{1,0:T(8,128)(2,1)}, u32[]{:S(2)}) copy-start(bf16[3456,256]{1,0:T(8,128)(2,1)} %param.10) | copy-start | bytes 5308420
  74.0 65.5 %copy-start.2 = (f32[1024,128]{1,0:T(8,128)S(1)}, f32[1024,128]{1,0:T(8,128)}, u32[]{:S(2)}) copy-start(f32[1024,128]{1,0:T(8,128)} %get-tuple-element.220) | copy-start | bytes 1572868
  134.9 3.5 %copy-start.3 = (bf16[4,4,64,256]{3,2,1,0:T(8,128)(2,1)S(1)}, bf16[4,4,64,256]{3,2,1,0:T(8,128)(2,1)}, u32[]{:S(2)}) copy-start(bf16[4,4,64,256]{3,2,1,0:T(8,128)(2,1)} %get-tuple-element.163) | copy-start | bytes 1572868
Sparse Core Ops, SparseCore 0:
  55.7 79.1 reduce-scatter.2
  137.7 7.3 reduce-scatter.4
where the time goes:
time: 180 us
  waiting for transfers between devices  63.3 us (35%)
  blocking collectives  47.8 us (27%)
  matrix products  22.7 us (13%)
  between operations  15.4 us (9%)
  local copies, waits for them, and re-layouts  14.7 us (8%)
  starting transfers between devices  11.5 us (6%)
  other arithmetic  4.15 us (2%)
    reduce_scatter x1, waiting for transfers between devices, body(): lax.psum_scatter(lax.dot_general(patches, cot_flat, (((0,), (0,)), ((), (...  60.9 us
    psum x1, blocking collectives, body(): lax.psum((jnp.sum(grad_act * normed, axis=(0, 1, 2)), jnp.sum(grad_act, a...  31.9 us
    unnamed x1, blocking collectives  13.3 us
    dot_general x27, matrix products, body(): lax.dot_general(window, kernel_taps[tap_index], (((1,), (1,)), ((), ())),...  12.5 us
    dot_general x1, matrix products, body(): jnp.dot(patches, weight, preferred_element_type=jnp.float32)  6.34 us
    unnamed x46, local copies, waits for them, and re-layouts  6.22 us
    ppermute x2, starting transfers between devices, with_halo(): before = lax.ppermute(last, axis, up)  6.07 us
    slice x3, local copies, waits for them, and re-layouts, body(): cot_padded[2 - lag_t:2 - lag_t + frame_count, 2 - row_off:2 - row_off + r...  5.01 us
  transfers between devices with their start and end apart: 8, of which 2 were waited for; matrix products, arithmetic and copies ran while one was open for 19% of the time, Pallas kernels for 0%

commit v1 on v0

--- a/solution.py
+++ b/solution.py
@@ -120,8 +120,11 @@
     grad_hidden = grad_hidden.reshape(frame_count, row_count, col_count, chan_in)
     grad_act = grad_hidden * sigma * (1.0 + act * (1.0 - sigma))
     grad_gain, grad_bias = lax.psum(
-        (jnp.sum(grad_act * normed, axis=(0, 1, 2)), jnp.sum(grad_act, axis=(0, 1, 2))),
-        ("tm", "dp", "width"),
+        lax.psum(
+            (jnp.sum(grad_act * normed, axis=(0, 1, 2)), jnp.sum(grad_act, axis=(0, 1, 2))),
+            ("dp", "width"),
+        ),
+        "tm",
     )
     cot_flat = cot_local.reshape(-1, chan_out)
     partial_rows = lax.psum_scatter(

time: 180 us -> 165 us (0.917)
  blocking collectives: 47.8 us -> 32.9 us
    psum x1, blocking collectives: 31.9 us -> 6.24 us  [body(): lax.psum((jnp.sum(grad_act * normed, axis=(0, 1, 2)), jnp.sum(grad_act, a...]
    psum x0 -> x1, blocking collectives: none -> 10.8 us  [body(): lax.psum(lax.psum((jnp.sum(grad_act * normed, axis=(0, 1, 2)), jnp.sum(gr...]
  transfers between devices with their start and end apart: 8 -> 8, of which waited for: 2 -> 2; matrix products, arithmetic and copies ran while one was open for 19% -> 20% of each run, Pallas kernels for 0% -> 0%
where the time goes in v1:
time: 165 us
  waiting for transfers between devices  63.3 us (38%)
  blocking collectives  32.9 us (20%)
  matrix products  22.7 us (14%)
  between operations  15.4 us (9%)
  local copies, waits for them, and re-layouts  14.7 us (9%)
  starting transfers between devices  11.5 us (7%)
  other arithmetic  4.15 us (3%)
    reduce_scatter x1, waiting for transfers between devices, body(): lax.psum_scatter(lax.dot_general(patches, cot_flat, (((0,), (0,)), ((), (...  60.9 us
    unnamed x1, blocking collectives  13.3 us
    dot_general x27, matrix products, body(): lax.dot_general(window, kernel_taps[tap_index], (((1,), (1,)), ((), ())),...  12.5 us
    psum x1, blocking collectives, body(): lax.psum(lax.psum((jnp.sum(grad_act * normed, axis=(0, 1, 2)), jnp.sum(gr...  10.8 us
    dot_general x1, matrix products, body(): jnp.dot(patches, weight, preferred_element_type=jnp.float32)  6.34 us
    psum x1, blocking collectives, body(): lax.psum((jnp.sum(grad_act * normed, axis=(0, 1, 2)), jnp.sum(grad_act, a...  6.24 us
    unnamed x46, local copies, waits for them, and re-layouts  6.22 us
    ppermute x2, starting transfers between devices, with_halo(): before = lax.ppermute(last, axis, up)  6.07 us
  transfers between devices with their start and end apart: 8, of which 2 were waited for; matrix products, arithmetic and copies ran while one was open for 20% of the time, Pallas kernels for 0%

profile of v1, /device:TPU:0, one launch (start us, length us, event | category | flops | bytes accessed | tf_op | source)
XLA Modules:
  0.0 164.7 jit_solution(473734962912098783)
XLA Ops:
  8.8 2.6 %all-reduce.7 = (f32[4,32]{1,0:T(4,128)S(1)}, f32[4,32]{1,0:T(4,128)S(1)}) all-reduce(f32[4,32]{1,0:T(4,128)S(1)} %reduce_sum.70, f32[4,32]{1,0:T(4,128)S(1)} %reduce_sum.74), channel_id=1, replica_groups=mesh['groups'=2,'tm'=4,'dp'=2,'width'=2] {'width'}, use_global_device_ids=true, to_apply=%region_2.0 | all-reduce | flops 256 | bytes 2048 | tf_op jit(solution)/shard_map/psum | solution.py:55
  11.4 1.2 dynamic-slice
  13.8 13.3 %all-reduce.6 = (f32[128]{0:T(128)S(1)}, f32[128]{0:T(128)S(1)}) all-reduce(f32[128]{0:T(128)S(1)} %dynamic-update-slice, f32[128]{0:T(128)S(1)} %dynamic-update-slice.1), channel_id=2, replica_groups=mesh['groups'=2,'tm'=4,'dp'=2,'width'=2] {'tm'}, use_global_device_ids=true, to_apply=%add.2 | all-reduce | flops 256 | bytes 2048
  27.8 1.2 multiply_convert_fusion.1
  29.0 1.3 collective-permute-start.1
  30.3 3.0 %collective-permute-start = (bf16[4,1,64,128]{3,2,1,0:T(8,128)(2,1)S(1)}, bf16[4,1,64,128]{3,2,1,0:T(8,128)(2,1)S(1)}, u32[]{:S(2)}, u32[]{:S(2)}) collective-permute-start(bf16[4,1,64,128]{3,2,1,0:T(8,128)(2,1)S(1)} %get-tuple-element.219), channel_id=1, source_target_pairs={{0,1},{2,3},{4,5},{6,7},{8,9},{10,11},{12,13},{14,15},{16,17},{18,... | collective-permute-start | bytes 196616 | tf_op jit(solution)/shard_map/ppermute | solution.py:30
  34.4 1.3 collective-permute-start.4
  35.7 3.0 %collective-permute-start.3 = (bf16[4,1,64,256]{3,2,1,0:T(8,128)(2,1)S(1)}, bf16[4,1,64,256]{3,2,1,0:T(8,128)(2,1)S(1)}, u32[]{:S(2)}, u32[]{:S(2)}) collective-permute-start(bf16[4,1,64,256]{3,2,1,0:T(8,128)(2,1)S(1)} %get-tuple-element.215), channel_id=1, source_target_pairs={{0,1},{2,3},{4,5},{6,7},{8,9},{10,11},{12,13},{14,15},{16,17},{18,... | collective-permute-start | bytes 393224 | tf_op jit(solution)/shard_map/ppermute | solution.py:30
  38.8 1.3 collective-permute-start.2
  40.2 1.3 collective-permute-start.5
  41.6 2.4 %collective-permute-done.2 = bf16[2,6,64,128]{3,2,1,0:T(8,128)(2,1)S(1)} collective-permute-done((bf16[2,6,64,128]{3,2,1,0:T(8,128)(2,1)S(1)}, bf16[2,6,64,128]{3,2,1,0:T(8,128)(2,1)S(1)}, u32[]{:S(2)}, u32[]{:S(2)}) %collective-permute-start.2) | collective-permute-done | bytes 196640 | tf_op jit(solution)/shard_map/ppermute | solution.py:39
  48.7 2.9 %copy-done.5 = bf16[1024,3456]{1,0:T(8,128)(2,1)} copy-done((bf16[1024,3456]{1,0:T(8,128)(2,1)}, bf16[1024,3456]{1,0:T(8,128)(2,1)S(1)}, u32[]{:S(2)}) %copy-start.5) | copy-done | bytes 7077912
  51.6 3.9 %fusion.43 = f32[3456,256]{1,0:T(8,128)} fusion(bf16[1024,3456]{1,0:T(8,128)(2,1)S(1)} %constant_dynamic-update-slice_fusion, bf16[1024,256]{1,0:T(8,128)(2,1)S(1)} %bitcast.120), kind=kOutput, calls=%fused_computation.158 | convolution fusion | flops 1811939328 | bytes 11141120 | tf_op jit(solution)/shard_map/dot_general | solution.py:131
  55.8 6.3 %convolution_convert_fusion = bf16[1024,256]{1,0:T(8,128)(2,1)} fusion(bf16[1024,3456]{1,0:T(8,128)(2,1)} %copy-done.5, bf16[3456,256]{1,0:T(8,128)(2,1)} %param.10), kind=kOutput, calls=%fused_computation.4 | convolution fusion | flops 1812201472 | bytes 9371648 | tf_op jit(solution)/shard_map/dot_general | solution.py:95
  62.3 2.6 %pad_slice_fusion.20 = (bf16[4,4,64,256]{3,2,1,0:T(8,128)(2,1)S(1)}, bf16[4,4,64,256]{3,2,1,0:T(8,128)(2,1)S(1)}, bf16[4,4,64,256]{3,2,1,0:T(8,128)(2,1)S(1)}, b...) fusion(bf16[6,6,64,256]{3,2,1,0:T(8,128)(2,1)S(1)} %pad_maximum, ...), kind=kLoop, calls=%fused_computation.137 | loop fusion | bytes 8519680 | tf_op jit(solution)/shard_map/slice | solution.py:109
  66.1 2.1 %pad_slice_fusion.19 = (bf16[4,4,64,256]{3,2,1,0:T(8,128)(2,1)}, bf16[4,4,64,256]{3,2,1,0:T(8,128)(2,1)S(1)}, bf16[4,4,64,256]{3,2,1,0:T(8,128)(2,1)S(1)}, bf16[...) fusion(bf16[6,6,64,256]{3,2,1,0:T(8,128)(2,1)S(1)} %pad_maximum, ...), kind=kLoop, calls=%fused_computation.136 | loop fusion | bytes 6946816 | tf_op jit(solution)/shard_map/slice | solution.py:109
  74.0 60.9 %reduce-scatter.3.cloned.1.call-done = f32[432,256]{1,0:T(8,128)} async-done(((f32[3456,256]{1,0:T(8,128)}), f32[432,256]{1,0:T(8,128)}) %reduce-scatter.3.cloned.1.call-update) | async-done | bytes 442384 | tf_op jit(solution)/shard_map/reduce_scatter | solution.py:130
  134.9 1.2 fusion.8
  136.1 1.1 convolution_add_fusion.3
  137.2 1.1 convolution_add_fusion.2
  138.4 1.1 convolution_add_fusion.1
  139.5 1.3 fusion.38
  140.8 6.2 %all-reduce.4 = (f32[128]{0:T(128)S(1)}, f32[128]{0:T(128)S(1)}) all-reduce(f32[128]{0:T(128)S(1)} %get-tuple-element.138, f32[128]{0:T(128)S(1)} %get-tuple-element.137), channel_id=1, replica_groups=mesh['groups'=2,'tm'=4,'dp'=2,'width'=2] {'dp','width'}, use_global_device_ids=true, to_apply=%region_15.16 | all-reduce | flops 256 | bytes 2048 | tf_op jit(solution)/shard_map/psum | solution.py:123
  147.1 10.8 %all-reduce.5 = (f32[128]{0:T(128)}, f32[128]{0:T(128)}) all-reduce(f32[128]{0:T(128)S(1)} %get-tuple-element.153, f32[128]{0:T(128)S(1)} %get-tuple-element.154), channel_id=1, replica_groups=mesh['groups'=2,'tm'=4,'dp'=2,'width'=2] {'tm'}, use_global_device_ids=true, to_apply=%region_16.17 | all-reduce | flops 256 | bytes 2048 | tf_op jit(solution)/shard_map/psum | solution.py:122
  (113 shorter events, 15.8 us)
Async XLA Ops:
  7.2 33.0 %copy-start = (bf16[1,4,4,64,256]{4,3,2,1,0:T(8,128)(2,1)S(1)}, bf16[1,4,4,64,256]{4,3,2,1,0:T(8,128)(2,1)}, u32[]{:S(2)}) copy-start(bf16[1,4,4,64,256]{4,3,2,1,0:T(8,128)(2,1)} %param.11) | copy-start | bytes 1572868
  7.2 127.7 %reduce-scatter.3.cloned.1.call-start = ((), (), s32[]{:S(2)}) async-start(), calls=%async_computation.2 | async-start | bytes 3981312 | tf_op jit(solution)/shard_map/reduce_scatter | solution.py:130
  29.0 9.7 %collective-permute-start.1 = (bf16[4,1,64,128]{3,2,1,0:T(8,128)(2,1)S(1)}, bf16[4,1,64,128]{3,2,1,0:T(8,128)(2,1)S(1)}, u32[]{:S(2)}, u32[]{:S(2)}) collective-permute-start(bf16[4,1,64,128]{3,2,1,0:T(8,128)(2,1)S(1)} %get-tuple-element.220), channel_id=1, source_target_pairs={{1,0},{3,2},{5,4},{7,6},{9,8},{11,10},{13,12},{15,14},{17,16},{19,... | collective-permute-start | bytes 196616 | tf_op jit(solution)/shard_map/ppermute | solution.py:31
  30.3 8.4 %collective-permute-start = (bf16[4,1,64,128]{3,2,1,0:T(8,128)(2,1)S(1)}, bf16[4,1,64,128]{3,2,1,0:T(8,128)(2,1)S(1)}, u32[]{:S(2)}, u32[]{:S(2)}) collective-permute-start(bf16[4,1,64,128]{3,2,1,0:T(8,128)(2,1)S(1)} %get-tuple-element.219), channel_id=1, source_target_pairs={{0,1},{2,3},{4,5},{6,7},{8,9},{10,11},{12,13},{14,15},{16,17},{18,... | collective-permute-start | bytes 196616 | tf_op jit(solution)/shard_map/ppermute | solution.py:30
  34.4 5.8 %collective-permute-start.4 = (bf16[4,1,64,256]{3,2,1,0:T(8,128)(2,1)S(1)}, bf16[4,1,64,256]{3,2,1,0:T(8,128)(2,1)S(1)}, u32[]{:S(2)}, u32[]{:S(2)}) collective-permute-start(bf16[4,1,64,256]{3,2,1,0:T(8,128)(2,1)S(1)} %get-tuple-element.216), channel_id=1, source_target_pairs={{1,0},{3,2},{5,4},{7,6},{9,8},{11,10},{13,12},{15,14},{17,16},{19,... | collective-permute-start | bytes 393224 | tf_op jit(solution)/shard_map/ppermute | solution.py:31
  35.7 4.5 %collective-permute-start.3 = (bf16[4,1,64,256]{3,2,1,0:T(8,128)(2,1)S(1)}, bf16[4,1,64,256]{3,2,1,0:T(8,128)(2,1)S(1)}, u32[]{:S(2)}, u32[]{:S(2)}) collective-permute-start(bf16[4,1,64,256]{3,2,1,0:T(8,128)(2,1)S(1)} %get-tuple-element.215), channel_id=1, source_target_pairs={{0,1},{2,3},{4,5},{6,7},{8,9},{10,11},{12,13},{14,15},{16,17},{18,... | collective-permute-start | bytes 393224 | tf_op jit(solution)/shard_map/ppermute | solution.py:30
  38.8 5.3 %collective-permute-start.2 = (bf16[2,6,64,128]{3,2,1,0:T(8,128)(2,1)S(1)}, bf16[2,6,64,128]{3,2,1,0:T(8,128)(2,1)S(1)}, u32[]{:S(2)}, u32[]{:S(2)}) collective-permute-start(bf16[2,6,64,128]{3,2,1,0:T(8,128)(2,1)S(1)} %pad_maximum_fusion.7), channel_id=1, source_target_pairs={{0,4},{4,8},{8,12},{1,5},{5,9},{9,13},{2,6},{6,10},{10,14},{3,7},{... | collective-permute-start | bytes 589832 | tf_op jit(solution)/shard_map/ppermute | solution.py:39
  40.2 21.9 %collective-permute-start.5 = (bf16[2,6,64,256]{3,2,1,0:T(8,128)(2,1)S(1)}, bf16[2,6,64,256]{3,2,1,0:T(8,128)(2,1)S(1)}, u32[]{:S(2)}, u32[]{:S(2)}) collective-permute-start(bf16[2,6,64,256]{3,2,1,0:T(8,128)(2,1)S(1)} %pad_maximum_fusion.3), channel_id=1, source_target_pairs={{4,0},{8,4},{12,8},{5,1},{9,5},{13,9},{6,2},{10,6},{14,10},{7,3},{... | collective-permute-start | bytes 1179656 | tf_op jit(solution)/shard_map/ppermute | solution.py:39
  46.4 1.0 copy-start.1
  46.4 1.0 copy-start.6
  46.4 1.0 copy-start.7
  48.7 2.9 %copy-start.5 = (bf16[1024,3456]{1,0:T(8,128)(2,1)}, bf16[1024,3456]{1,0:T(8,128)(2,1)S(1)}, u32[]{:S(2)}) copy-start(bf16[1024,3456]{1,0:T(8,128)(2,1)S(1)} %constant_dynamic-update-slice_fusion) | copy-start | bytes 21233668
  55.6 102.3 %reduce-scatter.5.cloned.1.call-start = ((), (), s32[]{:S(2)}) async-start(), calls=%async_computation.3 | async-start | bytes 663552 | tf_op jit(solution)/shard_map/reduce_scatter | solution.py:138
  62.3 2.7 %copy-start.4 = (bf16[3456,256]{1,0:T(8,128)(2,1)S(1)}, bf16[3456,256]{1,0:T(8,128)(2,1)}, u32[]{:S(2)}) copy-start(bf16[3456,256]{1,0:T(8,128)(2,1)} %param.10) | copy-start | bytes 5308420
  74.0 65.5 %copy-start.2 = (f32[1024,128]{1,0:T(8,128)S(1)}, f32[1024,128]{1,0:T(8,128)}, u32[]{:S(2)}) copy-start(f32[1024,128]{1,0:T(8,128)} %get-tuple-element.222) | copy-start | bytes 1572868
  134.9 3.5 %copy-start.3 = (bf16[4,4,64,256]{3,2,1,0:T(8,128)(2,1)S(1)}, bf16[4,4,64,256]{3,2,1,0:T(8,128)(2,1)}, u32[]{:S(2)}) copy-start(bf16[4,4,64,256]{3,2,1,0:T(8,128)(2,1)} %get-tuple-element.165) | copy-start | bytes 1572868
Sparse Core Ops, SparseCore 0:
  55.7 79.1 reduce-scatter.2
  137.7 7.3 reduce-scatter.4
